TPU v7x, 32 devices: a whole 2x2x4 slice. The times are simulated.
32 devices in a mesh: seq: 8 (over z, y), head: 4 (over x, core).
Axes of the slice: x: 2, y: 2, z: 4, core: 2. Of those that a mesh axis runs over, the one named last changes fastest.
Arguments:
- layer_input: bfloat16 [4096, 768], P('seq', 'head'), may hold values from -6 to 6
- ln1_gain: float32 [768], replicated, may hold values from 0.5 to 1.5
- ln1_bias: float32 [768], replicated, may hold values from -3 to 3
- w_query: bfloat16 [768, 768], P(None, 'head'), may hold values from -0.21875 to 0.21875
- b_query: float32 [768], P('head'), may hold values from -3 to 3
- w_key: bfloat16 [768, 768], P(None, 'head'), may hold values from -0.3125 to 0.3125
- w_value: bfloat16 [768, 768], P(None, 'head'), may hold values from -0.21875 to 0.21875
- b_value: float32 [768], P('head'), may hold values from -1.2 to 1.2
- sub_gain: float32 [768], P('head'), may hold values from 0.5 to 1.5
- sub_bias: float32 [768], P('head'), may hold values from -3 to 3
- w_out: bfloat16 [768, 768], P('head'), may hold values from -0.21875 to 0.21875
- b_out: float32 [768], replicated, may hold values from -3 to 3
- ln2_gain: float32 [768], replicated, may hold values from 0.5 to 1.5
- ln2_bias: float32 [768], replicated, may hold values from -3 to 3
- w_up: bfloat16 [768, 3072], P(None, 'head'), may hold values from -0.21875 to 0.21875
- b_up: float32 [3072], P('head'), may hold values from -3 to 3
- w_down: bfloat16 [3072, 768], P('head'), may hold values from -0.109375 to 0.109375
- b_down: float32 [768], replicated, may hold values from -3 to 3
- cotangent: bfloat16 [4096, 768], P('seq', 'head'), may hold values from -6 to 6
- row_lengths: int32 [6], replicated, may hold values from 1 to 3072, 4096 in all
Outputs:
- layer_output: bfloat16 [4096, 768], P('seq', 'head')
- grad_input: float32 [4096, 768], P('seq', 'head')
- grad_ln1_gain: float32 [768], replicated
- grad_ln1_bias: float32 [768], replicated
- grad_w_query: float32 [768, 768], P(None, 'head')
- grad_b_query: float32 [768], P('head')
- grad_w_key: float32 [768, 768], P(None, 'head')
- grad_w_value: float32 [768, 768], P(None, 'head')
- grad_b_value: float32 [768], P('head')
- grad_sub_gain: float32 [768], P('head')
- grad_sub_bias: float32 [768], P('head')
- grad_w_out: float32 [768, 768], P('head')
- grad_b_out: float32 [768], replicated
- grad_ln2_gain: float32 [768], replicated
- grad_ln2_bias: float32 [768], replicated
- grad_w_up: float32 [768, 3072], P(None, 'head')
- grad_b_up: float32 [3072], P('head')
- grad_w_down: float32 [3072, 768], P('head')
- grad_b_down: float32 [768], replicated
Inputs may be any that keep to these rules, and one draw needn't show every extreme that they name: `row_lengths`: the 6 row lengths sum to 4096, and the longest is exactly 3072.
All inputs are finite; a program needn't handle non-finite values.
Results may differ from a plain program's by a relative error of at most 0.018.
Values may be sent and summed in bfloat16 or wider, within the bound.
No kernel may reach another device: no remote copies, remote signals or barrier semaphores. Data moves between devices by JAX's collectives and lax.ppermute only.
A program may use at most 256 MiB of HBM per device.

v0:
```python
import math
import jax
import jax.numpy as jnp
from jax import lax
from jax.sharding import PartitionSpec as P

HEAD_DIM = 64
SEG = 2048
eps = 1e-05
segment_scales = (1, 2, 4, 8, 16)
dilation_steps = (1, 2, 4, 6, 12)


def layer_norm(inputs, norm_gain, norm_bias):
    center = inputs - jnp.mean(inputs, axis=-1, keepdims=True)
    spread = jnp.mean(center * center, axis=-1, keepdims=True)
    return center * lax.rsqrt(spread + eps) * norm_gain + norm_bias


def token_places(positions, lengths):
    row_ends = jnp.cumsum(lengths)
    starts = row_ends - lengths
    row_of = jnp.sum((positions[:, None] >= row_ends[None, :]).astype(jnp.int32), axis=1)
    onehot = (row_of[:, None] == jnp.arange(lengths.shape[0], dtype=jnp.int32)[None, :]).astype(
        jnp.int32
    )
    row_place = positions - jnp.sum(onehot * starts[None, :], axis=1)
    return (row_of, row_place)


def pattern_count(head_ids, query_row, query_place, key_row, key_place):
    allowed = (query_row[:, None] == key_row[None, :]) & (
        key_place[None, :] <= query_place[:, None]
    )
    counted = jnp.zeros((head_ids.shape[0], query_row.shape[0], key_row.shape[0]), jnp.float32)
    for scale_factor, step_size in zip(segment_scales, dilation_steps):
        seg_width = SEG * scale_factor
        same_seg = allowed & (query_place[:, None] // seg_width == key_place[None, :] // seg_width)
        offset = head_ids % step_size
        query_on = (query_place % seg_width % step_size)[None, :] == offset[:, None]
        key_on = (key_place % seg_width % step_size)[None, :] == offset[:, None]
        counted = counted + (same_seg[None] & query_on[:, :, None] & key_on[:, None, :]).astype(
            jnp.float32
        )
    return counted


def fold_keys(running, pieces, queries, head_ids, query_row, query_place, lengths, score_scale):
    key_rows, values = pieces
    piece_rows = key_rows.shape[0]
    block_rows = math.gcd(piece_rows, 2048)
    local_heads = queries.shape[0]
    key_blocks = key_rows.reshape(piece_rows // block_rows, block_rows, local_heads, -1)
    value_blocks = values.reshape(piece_rows // block_rows, block_rows, local_heads, -1)
    offsets = jnp.arange(piece_rows // block_rows, dtype=jnp.int32) * block_rows

    def advance(status, element):
        highest, totals, running_sum = status
        key_blk, value_blk, block_first = element
        key_row, key_place = token_places(
            block_first + jnp.arange(block_rows, dtype=jnp.int32), lengths
        )
        counted = pattern_count(head_ids, query_row, query_place, key_row, key_place)
        scores = (
            jnp.einsum("hqd,khd->hqk", queries, key_blk, preferred_element_type=jnp.float32)
            * score_scale
        )
        masked = jnp.where(counted > 0, scores, -1e30)
        new_high = jnp.maximum(highest, jnp.max(masked, axis=-1))
        weights = counted * jnp.exp(masked - new_high[..., None])
        factor = jnp.exp(highest - new_high)
        totals = totals * factor + jnp.sum(weights, axis=-1)
        running_sum = running_sum * factor[..., None] + jnp.einsum(
            "hqk,khd->hqd",
            weights.astype(jnp.bfloat16),
            value_blk,
            preferred_element_type=jnp.float32,
        )
        return ((new_high, totals, running_sum), None)

    running, unused = lax.scan(advance, running, (key_blocks, value_blocks, offsets))
    return running


def shards(
    layer_input,
    ln1_gain,
    ln1_bias,
    w_query,
    b_query,
    w_key,
    w_value,
    b_value,
    sub_gain,
    sub_bias,
    w_out,
    b_out,
    ln2_gain,
    ln2_bias,
    w_up,
    b_up,
    w_down,
    b_down,
    cotangent,
    row_lengths,
):
    rows_local = layer_input.shape[0]
    slice_width = layer_input.shape[1]
    head_share = w_query.shape[1]
    local_heads = head_share // HEAD_DIM
    head_pos = lax.axis_index("head")
    seq_pos = lax.axis_index("seq")
    full_width = head_share * lax.axis_size("head")
    score_scale = HEAD_DIM ** (-0.5)
    head_ids = head_pos * local_heads + jnp.arange(local_heads, dtype=jnp.int32)
    own_index = seq_pos * rows_local + jnp.arange(rows_local, dtype=jnp.int32)
    query_row, query_place = token_places(own_index, row_lengths)
    input_whole = lax.all_gather(layer_input, "head", axis=1, tiled=True).astype(jnp.float32)
    normed = layer_norm(input_whole, ln1_gain, ln1_bias).astype(jnp.bfloat16)
    queries = (jnp.dot(normed, w_query, preferred_element_type=jnp.float32) + b_query).astype(
        jnp.bfloat16
    )
    key_rows = jnp.dot(normed, w_key, preferred_element_type=jnp.float32).astype(jnp.bfloat16)
    values = (jnp.dot(normed, w_value, preferred_element_type=jnp.float32) + b_value).astype(
        jnp.bfloat16
    )
    query_heads = queries.reshape(rows_local, local_heads, HEAD_DIM).transpose(1, 0, 2)
    start_state = (
        jnp.full((local_heads, rows_local), -1e30, jnp.float32),
        jnp.zeros((local_heads, rows_local), jnp.float32),
        jnp.zeros((local_heads, rows_local, HEAD_DIM), jnp.float32),
    )
    highest, totals, running_sum = fold_keys(
        start_state,
        (
            lax.all_gather(key_rows, "seq", axis=0, tiled=True),
            lax.all_gather(values, "seq", axis=0, tiled=True),
        ),
        query_heads,
        head_ids,
        query_row,
        query_place,
        row_lengths,
        score_scale,
    )
    attended = running_sum / totals[..., None]
    log_total = highest + jnp.log(totals)
    mixed_heads = attended.transpose(1, 0, 2).reshape(rows_local, head_share)
    row_sum, row_square = lax.psum(
        (jnp.sum(mixed_heads, axis=1), jnp.sum(mixed_heads * mixed_heads, axis=1)), "head"
    )
    mean_value = row_sum / full_width
    inv_std = lax.rsqrt(row_square / full_width - mean_value * mean_value + eps)
    centered = (mixed_heads - mean_value[:, None]) * inv_std[:, None]
    sub_out = (centered * sub_gain + sub_bias).astype(jnp.bfloat16)
    projected = lax.psum_scatter(
        jnp.dot(sub_out, w_out, preferred_element_type=jnp.float32).astype(jnp.bfloat16),
        "head",
        scatter_dimension=1,
        tiled=True,
    ).astype(jnp.float32)
    out_bias_share = lax.dynamic_slice_in_dim(b_out, head_pos * slice_width, slice_width, 0)
    middle = layer_input.astype(jnp.float32) + (projected + out_bias_share)
    middle_whole = lax.all_gather(middle.astype(jnp.bfloat16), "head", axis=1, tiled=True).astype(
        middle.dtype
    )
    normed_mid = layer_norm(middle_whole, ln2_gain, ln2_bias).astype(jnp.bfloat16)
    inner_act = jnp.dot(normed_mid, w_up, preferred_element_type=jnp.float32) + b_up
    active = jax.nn.gelu(inner_act, approximate=False).astype(jnp.bfloat16)
    ffn_out = lax.psum_scatter(
        jnp.dot(active, w_down, preferred_element_type=jnp.float32).astype(jnp.bfloat16),
        "head",
        scatter_dimension=1,
        tiled=True,
    ).astype(jnp.float32)
    down_bias_share = lax.dynamic_slice_in_dim(b_down, head_pos * slice_width, slice_width, 0)
    layer_output = (middle + (ffn_out + down_bias_share)).astype(jnp.bfloat16)
    grad_whole = lax.all_gather(cotangent, "head", axis=1, tiled=True)
    grad_float = grad_whole.astype(jnp.float32)
    grad_w_down = jnp.dot(active.T, grad_whole, preferred_element_type=jnp.float32)
    grad_b_down = jnp.sum(grad_float, axis=0)
    grad_active = jnp.dot(grad_whole, w_down.T, preferred_element_type=jnp.float32)
    unused, gelu_back = jax.vjp(lambda inputs: jax.nn.gelu(inputs, approximate=False), inner_act)
    grad_inner = gelu_back(grad_active)[0].astype(jnp.bfloat16)
    grad_w_up = jnp.dot(normed_mid.T, grad_inner, preferred_element_type=jnp.float32)
    grad_b_up = jnp.sum(grad_inner.astype(jnp.float32), axis=0)
    grad_norm_mid = lax.psum(
        jnp.dot(grad_inner, w_up.T, preferred_element_type=jnp.float32).astype(jnp.bfloat16), "head"
    ).astype(jnp.float32)
    unused, mid_back = jax.vjp(layer_norm, middle_whole, ln2_gain, ln2_bias)
    grad_mid_norm, grad_ln2_gain, grad_ln2_bias = mid_back(grad_norm_mid)
    grad_middle = grad_float + grad_mid_norm
    grad_branch = grad_middle.astype(jnp.bfloat16)
    grad_b_out = jnp.sum(grad_branch.astype(jnp.float32), axis=0)
    grad_w_out = jnp.dot(sub_out.T, grad_branch, preferred_element_type=jnp.float32)
    grad_sub = jnp.dot(grad_branch, w_out.T, preferred_element_type=jnp.float32)
    grad_sub_gain = jnp.sum(grad_sub * centered, axis=0)
    grad_sub_bias = jnp.sum(grad_sub, axis=0)
    grad_hat = grad_sub * sub_gain
    hat_sum, hat_cross = lax.psum(
        (jnp.sum(grad_hat, axis=1), jnp.sum(grad_hat * centered, axis=1)), "head"
    )
    grad_mixed = inv_std[:, None] * (
        grad_hat - hat_sum[:, None] / full_width - centered * hat_cross[:, None] / full_width
    )
    grad_heads = (
        grad_mixed.reshape(rows_local, local_heads, HEAD_DIM)
        .transpose(1, 0, 2)
        .astype(jnp.bfloat16)
    )
    dot_term = jnp.sum(grad_heads.astype(jnp.float32) * attended, axis=-1)
    key_all, value_all = (
        lax.all_gather(key_rows, "seq", axis=0, tiled=True),
        lax.all_gather(values, "seq", axis=0, tiled=True),
    )
    total_rows = key_all.shape[0]
    block_rows = math.gcd(total_rows, 2048)
    key_blocks = key_all.reshape(total_rows // block_rows, block_rows, local_heads, HEAD_DIM)
    value_blocks = value_all.reshape(total_rows // block_rows, block_rows, local_heads, HEAD_DIM)
    offsets = jnp.arange(total_rows // block_rows, dtype=jnp.int32) * block_rows

    def score_parts(
        query_blk, grad_blk, log_blk, dot_blk, q_row, q_place, key_blk, value_blk, k_row, k_place
    ):
        counted = pattern_count(head_ids, q_row, q_place, k_row, k_place)
        scores = (
            jnp.einsum("hqd,khd->hqk", query_blk, key_blk, preferred_element_type=jnp.float32)
            * score_scale
        )
        masked = jnp.where(counted > 0, scores, -1e30)
        weights_norm = counted * jnp.exp(masked - log_blk[..., None])
        grad_probs = jnp.einsum(
            "hqd,khd->hqk", grad_blk, value_blk, preferred_element_type=jnp.float32
        )
        grad_scores = (weights_norm * (grad_probs - dot_blk[..., None])).astype(jnp.bfloat16)
        return (weights_norm, grad_scores)

    def back_step(grad_query_sum, element):
        key_blk, value_blk, block_first = element
        key_row, key_place = token_places(
            block_first + jnp.arange(block_rows, dtype=jnp.int32), row_lengths
        )
        weights_norm, grad_scores = score_parts(
            query_heads,
            grad_heads,
            log_total,
            dot_term,
            query_row,
            query_place,
            key_blk,
            value_blk,
            key_row,
            key_place,
        )
        grad_query_sum = grad_query_sum + jnp.einsum(
            "hqk,khd->hqd", grad_scores, key_blk, preferred_element_type=jnp.float32
        )
        grad_value = jnp.einsum(
            "hqk,hqd->khd",
            weights_norm.astype(jnp.bfloat16),
            grad_heads,
            preferred_element_type=jnp.float32,
        )
        grad_key = jnp.einsum(
            "hqk,hqd->khd", grad_scores, query_heads, preferred_element_type=jnp.float32
        )
        key_terms = jnp.concatenate(
            [grad_key.reshape(block_rows, -1) * score_scale, grad_value.reshape(block_rows, -1)],
            axis=1,
        )
        return (grad_query_sum, key_terms)

    query_zero = jnp.zeros((local_heads, rows_local, HEAD_DIM), jnp.float32)
    grad_query_sum, key_terms = lax.scan(back_step, query_zero, (key_blocks, value_blocks, offsets))
    key_terms = key_terms.reshape(total_rows, 2 * head_share)
    kv_grads = lax.psum_scatter(key_terms, "seq", scatter_dimension=0, tiled=True)
    grad_keys = kv_grads[:, :head_share].astype(jnp.bfloat16)
    grad_values = kv_grads[:, head_share:].astype(jnp.bfloat16)
    grad_queries = (grad_query_sum * score_scale).transpose(1, 0, 2).reshape(rows_local, head_share)
    grad_queries = grad_queries.astype(jnp.bfloat16)
    grad_w_query = jnp.dot(normed.T, grad_queries, preferred_element_type=jnp.float32)
    grad_b_query = jnp.sum(grad_queries.astype(jnp.float32), axis=0)
    grad_w_key = jnp.dot(normed.T, grad_keys, preferred_element_type=jnp.float32)
    grad_w_value = jnp.dot(normed.T, grad_values, preferred_element_type=jnp.float32)
    grad_b_value = jnp.sum(grad_values.astype(jnp.float32), axis=0)
    grad_normed = (
        jnp.dot(grad_queries, w_query.T, preferred_element_type=jnp.float32)
        + jnp.dot(grad_keys, w_key.T, preferred_element_type=jnp.float32)
        + jnp.dot(grad_values, w_value.T, preferred_element_type=jnp.float32)
    )
    grad_normed = lax.psum(grad_normed.astype(jnp.bfloat16), "head").astype(jnp.float32)
    unused, input_back = jax.vjp(layer_norm, input_whole, ln1_gain, ln1_bias)
    grad_in_norm, grad_ln1_gain, grad_ln1_bias = input_back(grad_normed)
    grad_input_whole = grad_middle + grad_in_norm
    grad_input = lax.dynamic_slice_in_dim(grad_input_whole, head_pos * slice_width, slice_width, 1)
    summed = lax.psum(
        (
            grad_ln1_gain,
            grad_ln1_bias,
            grad_w_query,
            grad_b_query,
            grad_w_key,
            grad_w_value,
            grad_b_value,
            grad_sub_gain,
            grad_sub_bias,
            grad_w_out,
            grad_b_out,
            grad_ln2_gain,
            grad_ln2_bias,
            grad_w_up,
            grad_b_up,
            grad_w_down,
            grad_b_down,
        ),
        "seq",
    )
    return (layer_output, grad_input) + tuple(summed)


def solution(mesh):
    in_specs = (
        P("seq", "head"),
        P(),
        P(),
        P(None, "head"),
        P("head"),
        P(None, "head"),
        P(None, "head"),
        P("head"),
        P("head"),
        P("head"),
        P("head", None),
        P(),
        P(),
        P(),
        P(None, "head"),
        P("head"),
        P("head", None),
        P(),
        P("seq", "head"),
        P(),
    )
    out_specs = (
        P("seq", "head"),
        P("seq", "head"),
        P(),
        P(),
        P(None, "head"),
        P("head"),
        P(None, "head"),
        P(None, "head"),
        P("head"),
        P("head"),
        P("head"),
        P("head", None),
        P(),
        P(),
        P(),
        P(None, "head"),
        P("head"),
        P("head", None),
        P(),
    )
    return jax.shard_map(shards, mesh=mesh, in_specs=in_specs, out_specs=out_specs, check_vma=False)
```

profile of v0, /device:TPU:0, one launch (start us, length us, event | category | flops | bytes accessed | tf_op | source)
XLA Modules:
  0.0 842.9 jit_solution(17732856070422200237)
XLA Ops:
  7.3 10.4 %all_gather.17 = bf16[512,768]{0,1:T(8,128)(2,1)S(1)} all-gather(bf16[512,192]{0,1:T(8,128)(2,1)} %param.24), channel_id=1, replica_groups=mesh['seq'=8,'head'=4] {'head'}, dimensions={1}, use_global_device_ids=true | all-gather | bytes 983040 | tf_op jit(solution)/shard_map/all_gather | solution.py:118
  22.7 43.9 %all-gather.3.cloned.1.call-done = bf16[4096,192]{0,1:T(8,128)(2,1)} async-done(((bf16[512,192]{0,1:T(8,128)(2,1)}), bf16[4096,192]{0,1:T(8,128)(2,1)}) %all-gather.3.cloned.1.call-update) | async-done | bytes 1572880 | tf_op jit(solution)/shard_map/all_gather | solution.py:136
  71.2 41.5 %all-gather.5.cloned.1.call-done = bf16[4096,192]{0,1:T(8,128)(2,1)} async-done(((bf16[512,192]{0,1:T(8,128)(2,1)}), bf16[4096,192]{0,1:T(8,128)(2,1)}) %all-gather.5.cloned.1.call-update) | async-done | bytes 1572880 | tf_op jit(solution)/shard_map/all_gather | solution.py:137
  117.4 77.7 %while.42 = (s32[]{:T(128)}, f32[3,512]{1,0:T(4,128)S(1)}, f32[3,512]{1,0:T(4,128)}, f32[3,512,64]{1,2,0:T(8,128)}, s32[512]{0:T(512)S(1)}, /*index=5*/s32[2]{0:...) while((s32[]{:T(128)}, f32[3,512]{1,0:T(4,128)S(1)}, ...), condition=%wide.region_10.11_spmd.clone.clone.clone, body=%wide.region_5.10_spmd.clone.clone.clone.sunk | while | flops 955956864 | bytes 106965376 | solution.py:81
  125.2 12.1 %fusion.202 = (f32[3,512]{1,0:T(4,128)S(1)}, f32[3,2048,512]{2,1,0:T(8,128)}) fusion(f32[512,2048]{0,1:T(8,128)S(1)} %get-tuple-element.1711, pred[3,2048]{1,0:T(4,128)(4,1)S(1)} %broadcast_compare_fusion.38, pred[3,512]{1,0:T(4,128)(4,1)S(1)} %broadcast_compare_fusion.39, pred[512,2048]{0,1:T(8,128)(4,1)S(1)} %get-tuple-element.1716, ...), kind=kOutput, calls=%fused_computation.7.clone.1 | convolution fusion | flops 465566208 | bytes 22001668 | tf_op jit(solution)/shard_map/while/body/eval_jaxpr/hqd,khd->hqk/dot_general | solution.py:65
  137.4 16.7 %fusion.203 = (f32[3,512]{1,0:T(4,128)S(1)}, bf16[3,512,2048]{1,2,0:T(8,128)(2,1)S(1)}) fusion(f32[3,512]{1,0:T(4,128)S(1)} %select_maximum_fusion.2, f32[3,2048,512]{2,1,0:T(8,128)} %get-tuple-element.1730, pred[3,2048]{1,0:T(4,128)(4,1)S(1)} %broadcast_compare_fusion.38, pred[3,512]{1,0:T(4,128)(4,1)S(1)} %broadcast_compare_fusion.39, ...), kind=kLoop, calls=%fused_computation.388.clone.1 | loop fusion | flops 72350208 | bytes 27305984 | tf_op jit(solution)/shard_map/while/body/eval_jaxpr/reduce_sum | solution.py:72
  164.1 12.1 %fusion.202 = (f32[3,512]{1,0:T(4,128)S(1)}, f32[3,2048,512]{2,1,0:T(8,128)}) fusion(f32[512,2048]{0,1:T(8,128)S(1)} %get-tuple-element.1711, pred[3,2048]{1,0:T(4,128)(4,1)S(1)} %broadcast_compare_fusion.38, pred[3,512]{1,0:T(4,128)(4,1)S(1)} %broadcast_compare_fusion.39, pred[512,2048]{0,1:T(8,128)(4,1)S(1)} %get-tuple-element.1716, ...), kind=kOutput, calls=%fused_computation.7.clone.1 | convolution fusion | flops 465566208 | bytes 22001668 | tf_op jit(solution)/shard_map/while/body/eval_jaxpr/hqd,khd->hqk/dot_general | solution.py:65
  176.3 16.7 %fusion.203 = (f32[3,512]{1,0:T(4,128)S(1)}, bf16[3,512,2048]{1,2,0:T(8,128)(2,1)S(1)}) fusion(f32[3,512]{1,0:T(4,128)S(1)} %select_maximum_fusion.2, f32[3,2048,512]{2,1,0:T(8,128)} %get-tuple-element.1730, pred[3,2048]{1,0:T(4,128)(4,1)S(1)} %broadcast_compare_fusion.38, pred[3,512]{1,0:T(4,128)(4,1)S(1)} %broadcast_compare_fusion.39, ...), kind=kLoop, calls=%fused_computation.388.clone.1 | loop fusion | flops 72350208 | bytes 27305984 | tf_op jit(solution)/shard_map/while/body/eval_jaxpr/reduce_sum | solution.py:72
  196.4 6.0 all-reduce.3
  204.9 8.7 %all_gather.21 = bf16[512,768]{0,1:T(8,128)(2,1)S(1)} all-gather(bf16[512,192]{0,1:T(8,128)(2,1)} %param.42), channel_id=1, replica_groups=mesh['seq'=8,'head'=4] {'head'}, dimensions={1}, use_global_device_ids=true | all-gather | bytes 983040 | tf_op jit(solution)/shard_map/all_gather | solution.py:178
  213.6 11.9 %reduce-scatter.4.cloned.1.call-done = bf16[512,192]{0,1:T(8,128)(2,1)} async-done(((bf16[512,768]{0,1:T(8,128)(2,1)}), bf16[512,192]{0,1:T(8,128)(2,1)}) %reduce-scatter.4.cloned.1.call-update) | async-done | bytes 196624 | tf_op jit(solution)/shard_map/reduce_scatter | solution.py:156
  226.7 8.7 %all_gather.20 = bf16[512,768]{0,1:T(8,128)(2,1)S(1)} all-gather(bf16[512,192]{0,1:T(8,128)(2,1)S(1)} %fusion.114), channel_id=1, replica_groups=mesh['seq'=8,'head'=4] {'head'}, dimensions={1}, use_global_device_ids=true | all-gather | bytes 983040 | tf_op jit(solution)/shard_map/all_gather | solution.py:164
  246.1 34.5 %all-reduce.8.cloned.1.call-done = bf16[512,768]{0,1:T(8,128)(2,1)} async-done(((bf16[512,768]{0,1:T(8,128)(2,1)}), bf16[512,768]{0,1:T(8,128)(2,1)}) %all-reduce.8.cloned.1.call-update) | async-done | bytes 786448 | tf_op jit(solution)/shard_map/psum | solution.py:187
  289.1 6.5 all-reduce.2
  298.0 104.5 %while.43 = (s32[]{:T(128)}, f32[3,512,64]{1,2,0:T(8,128)S(1)}, f32[2,2048,384]{2,1,0:T(8,128)}, s32[512]{0:T(512)S(1)}, s32[2]{0:T(128)}, /*index=5*/s32[6,1]{0...) while((s32[]{:T(128)}, f32[3,512,64]{1,2,0:T(8,128)S(1)}, ...), condition=%wide.region_30.31_spmd.clone.clone.clone, body=%wide.region_27.30_spmd.clone.clone.clone.sunk | while | flops 2108366976 | bytes 175255120 | solution.py:274
  309.0 12.4 %fusion.216 = f32[3,512,2048]{1,2,0:T(8,128)S(1)} fusion(f32[3,512]{1,0:T(4,128)S(1)} %copy-done.86, f32[512,2048]{0,1:T(8,128)S(1)} %get-tuple-element.1766, pred[3,2048]{1,0:T(4,128)(4,1)S(1)} %broadcast_compare_fusion.46, pred[3,512]{1,0:T(4,128)(4,1)S(1)} %broadcast_compare_fusion.47, pred[512,2048]{0,1:T(8,128)(4,1)S(1)} %get-tuple-element.1771, ...), kind=kOutput, calls=%fused_computation.139.clone.1 | convolution fusion | flops 468713472 | bytes 22003716 | tf_op jit(solution)/shard_map/while/body/eval_jaxpr/hqd,khd->hqk/dot_general | solution.py:227
  332.3 6.7 fusion.218
  361.2 12.4 %fusion.216 = f32[3,512,2048]{1,2,0:T(8,128)S(1)} fusion(f32[3,512]{1,0:T(4,128)S(1)} %copy-done.86, f32[512,2048]{0,1:T(8,128)S(1)} %get-tuple-element.1766, pred[3,2048]{1,0:T(4,128)(4,1)S(1)} %broadcast_compare_fusion.46, pred[3,512]{1,0:T(4,128)(4,1)S(1)} %broadcast_compare_fusion.47, pred[512,2048]{0,1:T(8,128)(4,1)S(1)} %get-tuple-element.1771, ...), kind=kOutput, calls=%fused_computation.139.clone.1 | convolution fusion | flops 468713472 | bytes 22003716 | tf_op jit(solution)/shard_map/while/body/eval_jaxpr/hqd,khd->hqk/dot_general | solution.py:227
  384.5 6.7 fusion.218
  417.4 103.4 %reduce-scatter.8.cloned.1.call-done = f32[512,384]{1,0:T(8,128)} async-done(((f32[4096,384]{1,0:T(8,128)}), f32[512,384]{1,0:T(8,128)}) %reduce-scatter.8.cloned.1.call-update) | async-done | bytes 786448 | tf_op jit(solution)/shard_map/reduce_scatter | solution.py:276
  531.6 14.2 %reduce-scatter.6.cloned.1.call-done = bf16[512,192]{0,1:T(8,128)(2,1)} async-done(((bf16[512,768]{0,1:T(8,128)(2,1)}), bf16[512,192]{0,1:T(8,128)(2,1)}) %reduce-scatter.6.cloned.1.call-update) | async-done | bytes 196624 | tf_op jit(solution)/shard_map/reduce_scatter | solution.py:170
  549.4 33.4 %all-reduce.10.cloned.1.call-done = bf16[512,768]{0,1:T(8,128)(2,1)} async-done(((bf16[512,768]{0,1:T(8,128)(2,1)}), bf16[512,768]{0,1:T(8,128)(2,1)}) %all-reduce.10.cloned.1.call-update) | async-done | bytes 786448 | tf_op jit(solution)/shard_map/psum | solution.py:291
  585.3 40.1 %all-reduce = (f32[768]{0:T(1024)}, f32[768]{0:T(1024)}, f32[192]{0:T(256)}, f32[192]{0:T(256)}, f32[192]{0:T(256)}, /*index=5*/f32[192]{0:T(256)}, f32[768]{0:T...) all-reduce(f32[768]{0:T(1024)} %get-tuple-element.1251, ...), channel_id=1, replica_groups=mesh['seq'=8,'head'=4] {'seq'}, use_global_device_ids=true, to_apply=%region_36.37 | all-reduce | flops 6144 | bytes 49152 | tf_op jit(solution)/shard_map/psum | solution.py:296
  628.6 198.8 %all-reduce.12.cloned.1.call-done = (f32[768,192]{0,1:T(8,128)}, f32[768,192]{0,1:T(8,128)}, f32[768,192]{0,1:T(8,128)}, f32[192,768]{1,0:T(8,128)}, f32[768,768]{1,0:T(8,128)}, /*index=5*/f32[768,768]{1,0:T(8,128)}) async-done(((f32[768,192]{0,1:T(8,128)}, f32[768,192]{0,1:T(8,128)}, f32[768,192]{0,1:T(8,128)}, f32[192,768]{1,0:T(8,128)}, f32[768,768]{1,0:T(8,128)}, /*index=5*/f32[768,768]{1,0:T(8,128)}), ...) | async-done | bytes 7077904 | tf_op jit(solution)/shard_map/psum | solution.py:296
  (453 shorter events, 168.9 us)
Async XLA Ops:
  7.2 229.8 %copy-start = (bf16[768,768]{1,0:T(8,128)(2,1)S(1)}, bf16[768,768]{1,0:T(8,128)(2,1)}, u32[]{:S(2)}) copy-start(bf16[768,768]{1,0:T(8,128)(2,1)} %param.40) | copy-start | bytes 3538948
  7.2 59.4 %all-gather.3.cloned.1.call-start = ((), (), s32[]{:S(2)}) async-start(), calls=%async_computation.3 | async-start | bytes 1769472 | tf_op jit(solution)/shard_map/all_gather | solution.py:136
  20.3 92.5 %all-gather.5.cloned.1.call-start = ((), (), s32[]{:S(2)}) async-start(), calls=%async_computation.4 | async-start | bytes 1769472 | tf_op jit(solution)/shard_map/all_gather | solution.py:137
  21.4 204.1 %reduce-scatter.4.cloned.1.call-start = ((), (), s32[]{:S(2)}) async-start(), calls=%async_computation.5 | async-start | bytes 983040 | tf_op jit(solution)/shard_map/reduce_scatter | solution.py:156
  202.6 22.9 %copy-start.32 = (bf16[512,192]{0,1:T(8,128)(2,1)S(1)}, bf16[512,192]{0,1:T(8,128)(2,1)}, u32[]{:S(2)}) copy-start(bf16[512,192]{0,1:T(8,128)(2,1)} %param.24) | copy-start | bytes 589828
  204.0 76.6 %all-reduce.8.cloned.1.call-start = ((), (), s32[]{:S(2)}) async-start(), calls=%async_computation.7 | async-start | bytes 1572864 | tf_op jit(solution)/shard_map/psum | solution.py:187
  204.9 30.6 %copy-start.85 = (f32[192]{0:T(256)}, f32[192]{0:T(256)S(1)}, u32[]{:S(2)}) copy-start(f32[192]{0:T(256)S(1)} %dynamic_slice.65) | copy-start | bytes 2308
  213.5 23.4 %copy-start.23 = (bf16[512,768]{0,1:T(8,128)(2,1)}, bf16[512,768]{0,1:T(8,128)(2,1)S(1)}, u32[]{:S(2)}) copy-start(bf16[512,768]{0,1:T(8,128)(2,1)S(1)} %all_gather.21) | copy-start | bytes 2359300
  213.5 22.2 %copy-start.67 = (f32[768]{0:T(1024)S(1)}, f32[768]{0:T(1024)}, u32[]{:S(2)}) copy-start(f32[768]{0:T(1024)} %param.36) | copy-start | bytes 9220
  213.6 22.2 %copy-start.93 = (f32[768]{0:T(1024)S(1)}, f32[768]{0:T(1024)}, u32[]{:S(2)}) copy-start(f32[768]{0:T(1024)} %param.39) | copy-start | bytes 9220
  213.6 22.2 %copy-start.94 = (f32[768]{0:T(1024)S(1)}, f32[768]{0:T(1024)}, u32[]{:S(2)}) copy-start(f32[768]{0:T(1024)} %param.37) | copy-start | bytes 9220
  235.3 49.3 %copy-start.9 = (bf16[512,768]{0,1:T(8,128)(2,1)}, bf16[512,768]{0,1:T(8,128)(2,1)S(1)}, u32[]{:S(2)}) copy-start(bf16[512,768]{0,1:T(8,128)(2,1)S(1)} %all_gather.20) | copy-start | bytes 2359300
  235.5 49.1 %copy-start.65 = (f32[512]{0:T(512)}, f32[512]{0:T(512)S(1)}, u32[]{:S(2)}) copy-start(f32[512]{0:T(512)S(1)} %broadcast_multiply_fusion.1) | copy-start | bytes 6148
  235.8 48.8 %copy-start.74 = (f32[512]{0:T(512)}, f32[512]{0:T(512)S(1)}, u32[]{:S(2)}) copy-start(f32[512]{0:T(512)S(1)} %fusion.123) | copy-start | bytes 6148
  243.7 36.9 %copy-start.68 = (f32[768]{0:T(1024)S(1)}, f32[768]{0:T(1024)}, u32[]{:S(2)}) copy-start(f32[768]{0:T(1024)} %param.36) | copy-start | bytes 9220
  245.5 275.3 %reduce-scatter.8.cloned.1.call-start = ((), (), s32[]{:S(2)}) async-start(), calls=%async_computation.8 | async-start | bytes 7077888 | tf_op jit(solution)/shard_map/reduce_scatter | solution.py:276
  402.5 143.2 %reduce-scatter.6.cloned.1.call-start = ((), (), s32[]{:S(2)}) async-start(), calls=%async_computation.6 | async-start | bytes 983040 | tf_op jit(solution)/shard_map/reduce_scatter | solution.py:170
  411.2 171.6 %all-reduce.10.cloned.1.call-start = ((), (), s32[]{:S(2)}) async-start(), calls=%async_computation.9 | async-start | bytes 1572864 | tf_op jit(solution)/shard_map/psum | solution.py:291
  525.1 302.3 %all-reduce.12.cloned.1.call-start = ((), (), s32[]{:S(2)}) async-start(), calls=%async_computation.10 | async-start | bytes 14155776 | tf_op jit(solution)/shard_map/psum | solution.py:296
  528.8 54.0 %copy-start.64 = (f32[512]{0:T(512)S(1)}, f32[512]{0:T(512)}, u32[]{:S(2)}) copy-start(f32[512]{0:T(512)} %copy-done.63) | copy-start | bytes 6148
  528.8 54.0 %copy-start.71 = (f32[768]{0:T(1024)S(1)}, f32[768]{0:T(1024)}, u32[]{:S(2)}) copy-start(f32[768]{0:T(1024)} %param.25) | copy-start | bytes 9220
  528.8 54.0 %copy-start.73 = (f32[512]{0:T(512)S(1)}, f32[512]{0:T(512)}, u32[]{:S(2)}) copy-start(f32[512]{0:T(512)} %copy-done.72) | copy-start | bytes 6148
  528.8 54.0 %copy-start.12 = (bf16[512,768]{0,1:T(8,128)(2,1)S(1)}, bf16[512,768]{0,1:T(8,128)(2,1)}, u32[]{:S(2)}) copy-start(bf16[512,768]{0,1:T(8,128)(2,1)} %copy-done.11) | copy-start | bytes 2359300
  528.8 96.6 %copy-start.81 = (f32[512]{0:T(512)S(1)}, f32[512]{0:T(512)}, u32[]{:S(2)}) copy-start(f32[512]{0:T(512)} %copy-done.80) | copy-start | bytes 6148
  (111 other events, 622.1 us)
Sparse Core Ops, SparseCore 0:
  20.4 46.1 all-gather.2
  69.2 43.4 all-gather.4
  204.2 21.3 reduce-scatter.3
  245.6 34.9 all-reduce.7
  402.6 118.0 reduce-scatter.7
  523.3 22.3 reduce-scatter.5
  548.1 34.6 all-reduce.9
  589.6 237.7 all-reduce.11
where the time goes:
time: 852 us; the launch traced here: 843 us
  waiting for transfers between devices  482 us (57%)
  matrix products  120 us (14%)
  other arithmetic  95.7 us (11%)
  blocking collectives  80.4 us (9%)
  local copies, waits for them, and re-layouts  48.5 us (6%)
  between operations  15.1 us (2%)
    psum x1, waiting for transfers between devices, shards(): lax.psum((grad_ln1_gain, grad_ln1_bias, grad_w_query, grad_b_query, grad_...  199 us
    reduce_scatter x1, waiting for transfers between devices, shards(): lax.psum_scatter(key_terms, 'seq', scatter_dimension=0, tiled=True)  103 us
    all_gather x1, waiting for transfers between devices, shards(): lax.all_gather(key_rows, 'seq', axis=0, tiled=True)  43.9 us
    all_gather x1, waiting for transfers between devices, shards(): lax.all_gather(values, 'seq', axis=0, tiled=True)  41.5 us
    psum x1, blocking collectives, shards(): lax.psum((grad_ln1_gain, grad_ln1_bias, grad_w_query, grad_b_query, grad_...  40.1 us
    psum x1, waiting for transfers between devices, shards(): lax.psum(jnp.dot(grad_inner, w_up.T, preferred_element_type=jnp.float32)....  34.5 us
    psum x1, waiting for transfers between devices, shards(): lax.psum(grad_normed.astype(jnp.bfloat16), 'head').astype(jnp.float32)  33.4 us
    reduce_sum x2, other arithmetic, advance(): totals = totals * factor + jnp.sum(weights, axis=-1)  33.3 us
  transfers between devices with their start and end apart: 8, of which 8 were waited for; matrix products, arithmetic and copies ran while one was open for 5% of the time, Pallas kernels for 0%

commit v1 on v0

--- a/solution.py
+++ b/solution.py
@@ -9,6 +9,12 @@
 eps = 1e-05
 segment_scales = (1, 2, 4, 8, 16)
 dilation_steps = (1, 2, 4, 6, 12)
+
+
+def summed_here(x, axis):
+    pieces = lax.all_gather(x, axis, axis=0, tiled=False)
+    result = pieces.sum(axis=0)
+    return result
 
 
 def layer_norm(inputs, norm_gain, norm_bias):
@@ -288,7 +294,7 @@
         + jnp.dot(grad_keys, w_key.T, preferred_element_type=jnp.float32)
         + jnp.dot(grad_values, w_value.T, preferred_element_type=jnp.float32)
     )
-    grad_normed = lax.psum(grad_normed.astype(jnp.bfloat16), "head").astype(jnp.float32)
+    grad_normed = summed_here(grad_normed.astype(jnp.bfloat16), "head").astype(jnp.float32)
     unused, input_back = jax.vjp(layer_norm, input_whole, ln1_gain, ln1_bias)
     grad_in_norm, grad_ln1_gain, grad_ln1_bias = input_back(grad_normed)
     grad_input_whole = grad_middle + grad_in_norm

time: 852 us -> 846 us (level)
  waiting for transfers between devices: 482 us -> 472 us
    psum x1 -> x0, waiting for transfers between devices: 33.4 us -> none  [shards(): lax.psum(grad_normed.astype(jnp.bfloat16), 'head').astype(jnp.float32)]
    all_gather x0 -> x1, waiting for transfers between devices: none -> 27.6 us  [summed_here(): pieces = lax.all_gather(x, axis, axis=0, tiled=False)]
    unnamed x158 -> x178, local copies, waits for them, and re-layouts: 15.4 us -> 18.8 us
where the time goes in v1:
time: 846 us; the launch traced here: 836 us
  waiting for transfers between devices  472 us (56%)
  matrix products  117 us (14%)
  other arithmetic  97.2 us (11%)
  blocking collectives  80.9 us (10%)
  local copies, waits for them, and re-layouts  53 us (6%)
  between operations  15.2 us (2%)
    psum x1, waiting for transfers between devices, shards(): lax.psum((grad_ln1_gain, grad_ln1_bias, grad_w_query, grad_b_query, grad_...  192 us
    reduce_scatter x1, waiting for transfers between devices, shards(): lax.psum_scatter(key_terms, 'seq', scatter_dimension=0, tiled=True)  110 us
    all_gather x1, waiting for transfers between devices, shards(): lax.all_gather(key_rows, 'seq', axis=0, tiled=True)  43.9 us
    all_gather x1, waiting for transfers between devices, shards(): lax.all_gather(values, 'seq', axis=0, tiled=True)  41.5 us
    psum x1, blocking collectives, shards(): lax.psum((grad_ln1_gain, grad_ln1_bias, grad_w_query, grad_b_query, grad_...  40.6 us
    psum x1, waiting for transfers between devices, shards(): lax.psum(jnp.dot(grad_inner, w_up.T, preferred_element_type=jnp.float32)....  34.5 us
    reduce_sum x2, other arithmetic, advance(): totals = totals * factor + jnp.sum(weights, axis=-1)  33.3 us
    all_gather x1, waiting for transfers between devices, summed_here(): pieces = lax.all_gather(x, axis, axis=0, tiled=False)  27.6 us
  transfers between devices with their start and end apart: 8, of which 8 were waited for; matrix products, arithmetic and copies ran while one was open for 5% of the time, Pallas kernels for 0%

profile of v1, /device:TPU:0, one launch (start us, length us, event | category | flops | bytes accessed | tf_op | source)
XLA Modules:
  0.0 836.4 jit_solution(17438088587250301548)
XLA Ops:
  7.3 10.4 %all_gather.23 = bf16[512,768]{0,1:T(8,128)(2,1)S(1)} all-gather(bf16[512,192]{0,1:T(8,128)(2,1)} %param.24), channel_id=1, replica_groups=mesh['seq'=8,'head'=4] {'head'}, dimensions={1}, use_global_device_ids=true | all-gather | bytes 983040 | tf_op jit(solution)/shard_map/all_gather | solution.py:124
  22.8 43.9 %all-gather.5.cloned.1.call-done = bf16[4096,192]{0,1:T(8,128)(2,1)} async-done(((bf16[512,192]{0,1:T(8,128)(2,1)}), bf16[4096,192]{0,1:T(8,128)(2,1)}) %all-gather.5.cloned.1.call-update) | async-done | bytes 1572880 | tf_op jit(solution)/shard_map/all_gather | solution.py:142
  71.3 41.5 %all-gather.7.cloned.1.call-done = bf16[4096,192]{0,1:T(8,128)(2,1)} async-done(((bf16[512,192]{0,1:T(8,128)(2,1)}), bf16[4096,192]{0,1:T(8,128)(2,1)}) %all-gather.7.cloned.1.call-update) | async-done | bytes 1572880 | tf_op jit(solution)/shard_map/all_gather | solution.py:143
  117.4 77.7 %while.42 = (s32[]{:T(128)}, f32[3,512]{1,0:T(4,128)S(1)}, f32[3,512]{1,0:T(4,128)}, f32[3,512,64]{1,2,0:T(8,128)}, s32[512]{0:T(512)S(1)}, /*index=5*/s32[2]{0:...) while((s32[]{:T(128)}, f32[3,512]{1,0:T(4,128)S(1)}, ...), condition=%wide.region_10.11_spmd.clone.clone.clone, body=%wide.region_5.10_spmd.clone.clone.clone.sunk | while | flops 955956864 | bytes 106965376 | solution.py:87
  125.3 12.1 %fusion.202 = (f32[3,512]{1,0:T(4,128)S(1)}, f32[3,2048,512]{2,1,0:T(8,128)}) fusion(f32[512,2048]{0,1:T(8,128)S(1)} %get-tuple-element.1745, pred[3,2048]{1,0:T(4,128)(4,1)S(1)} %broadcast_compare_fusion.38, pred[3,512]{1,0:T(4,128)(4,1)S(1)} %broadcast_compare_fusion.39, pred[512,2048]{0,1:T(8,128)(4,1)S(1)} %get-tuple-element.1750, ...), kind=kOutput, calls=%fused_computation.7.clone.1 | convolution fusion | flops 465566208 | bytes 22001668 | tf_op jit(solution)/shard_map/while/body/eval_jaxpr/hqd,khd->hqk/dot_general | solution.py:71
  137.4 16.7 %fusion.203 = (f32[3,512]{1,0:T(4,128)S(1)}, bf16[3,512,2048]{1,2,0:T(8,128)(2,1)S(1)}) fusion(f32[3,512]{1,0:T(4,128)S(1)} %select_maximum_fusion.2, f32[3,2048,512]{2,1,0:T(8,128)} %get-tuple-element.1764, pred[3,2048]{1,0:T(4,128)(4,1)S(1)} %broadcast_compare_fusion.38, pred[3,512]{1,0:T(4,128)(4,1)S(1)} %broadcast_compare_fusion.39, ...), kind=kLoop, calls=%fused_computation.388.clone.1 | loop fusion | flops 72350208 | bytes 27305984 | tf_op jit(solution)/shard_map/while/body/eval_jaxpr/reduce_sum | solution.py:78
  164.2 12.1 %fusion.202 = (f32[3,512]{1,0:T(4,128)S(1)}, f32[3,2048,512]{2,1,0:T(8,128)}) fusion(f32[512,2048]{0,1:T(8,128)S(1)} %get-tuple-element.1745, pred[3,2048]{1,0:T(4,128)(4,1)S(1)} %broadcast_compare_fusion.38, pred[3,512]{1,0:T(4,128)(4,1)S(1)} %broadcast_compare_fusion.39, pred[512,2048]{0,1:T(8,128)(4,1)S(1)} %get-tuple-element.1750, ...), kind=kOutput, calls=%fused_computation.7.clone.1 | convolution fusion | flops 465566208 | bytes 22001668 | tf_op jit(solution)/shard_map/while/body/eval_jaxpr/hqd,khd->hqk/dot_general | solution.py:71
  176.3 16.7 %fusion.203 = (f32[3,512]{1,0:T(4,128)S(1)}, bf16[3,512,2048]{1,2,0:T(8,128)(2,1)S(1)}) fusion(f32[3,512]{1,0:T(4,128)S(1)} %select_maximum_fusion.2, f32[3,2048,512]{2,1,0:T(8,128)} %get-tuple-element.1764, pred[3,2048]{1,0:T(4,128)(4,1)S(1)} %broadcast_compare_fusion.38, pred[3,512]{1,0:T(4,128)(4,1)S(1)} %broadcast_compare_fusion.39, ...), kind=kLoop, calls=%fused_computation.388.clone.1 | loop fusion | flops 72350208 | bytes 27305984 | tf_op jit(solution)/shard_map/while/body/eval_jaxpr/reduce_sum | solution.py:78
  196.4 6.0 all-reduce.3
  204.9 8.7 %all_gather.27 = bf16[512,768]{0,1:T(8,128)(2,1)S(1)} all-gather(bf16[512,192]{0,1:T(8,128)(2,1)} %param.42), channel_id=1, replica_groups=mesh['seq'=8,'head'=4] {'head'}, dimensions={1}, use_global_device_ids=true | all-gather | bytes 983040 | tf_op jit(solution)/shard_map/all_gather | solution.py:184
  213.6 11.9 %reduce-scatter.4.cloned.1.call-done = bf16[512,192]{0,1:T(8,128)(2,1)} async-done(((bf16[512,768]{0,1:T(8,128)(2,1)}), bf16[512,192]{0,1:T(8,128)(2,1)}) %reduce-scatter.4.cloned.1.call-update) | async-done | bytes 196624 | tf_op jit(solution)/shard_map/reduce_scatter | solution.py:162
  226.7 8.7 %all_gather.26 = bf16[512,768]{0,1:T(8,128)(2,1)S(1)} all-gather(bf16[512,192]{0,1:T(8,128)(2,1)S(1)} %fusion.114), channel_id=1, replica_groups=mesh['seq'=8,'head'=4] {'head'}, dimensions={1}, use_global_device_ids=true | all-gather | bytes 983040 | tf_op jit(solution)/shard_map/all_gather | solution.py:170
  246.1 34.5 %all-reduce.7.cloned.1.call-done = bf16[512,768]{0,1:T(8,128)(2,1)} async-done(((bf16[512,768]{0,1:T(8,128)(2,1)}), bf16[512,768]{0,1:T(8,128)(2,1)}) %all-reduce.7.cloned.1.call-update) | async-done | bytes 786448 | tf_op jit(solution)/shard_map/psum | solution.py:193
  289.1 6.5 all-reduce.2
  298.0 104.7 %while.43 = (s32[]{:T(128)}, f32[3,512,64]{1,2,0:T(8,128)S(1)}, f32[2,2048,384]{2,1,0:T(8,128)}, s32[512]{0:T(512)S(1)}, s32[2]{0:T(128)}, /*index=5*/s32[6,1]{0...) while((s32[]{:T(128)}, f32[3,512,64]{1,2,0:T(8,128)S(1)}, ...), condition=%wide.region_30.31_spmd.clone.clone.clone, body=%wide.region_27.30_spmd.clone.clone.clone.sunk | while | flops 2108366976 | bytes 175255120 | solution.py:280
  309.1 12.4 %fusion.216 = f32[3,512,2048]{1,2,0:T(8,128)S(1)} fusion(f32[3,512]{1,0:T(4,128)S(1)} %copy-done.96, f32[512,2048]{0,1:T(8,128)S(1)} %get-tuple-element.1800, pred[3,2048]{1,0:T(4,128)(4,1)S(1)} %broadcast_compare_fusion.46, pred[3,512]{1,0:T(4,128)(4,1)S(1)} %broadcast_compare_fusion.47, pred[512,2048]{0,1:T(8,128)(4,1)S(1)} %get-tuple-element.1805, ...), kind=kOutput, calls=%fused_computation.139.clone.1 | convolution fusion | flops 468713472 | bytes 22003716 | tf_op jit(solution)/shard_map/while/body/eval_jaxpr/hqd,khd->hqk/dot_general | solution.py:233
  332.4 6.7 fusion.218
  361.4 12.4 %fusion.216 = f32[3,512,2048]{1,2,0:T(8,128)S(1)} fusion(f32[3,512]{1,0:T(4,128)S(1)} %copy-done.96, f32[512,2048]{0,1:T(8,128)S(1)} %get-tuple-element.1800, pred[3,2048]{1,0:T(4,128)(4,1)S(1)} %broadcast_compare_fusion.46, pred[3,512]{1,0:T(4,128)(4,1)S(1)} %broadcast_compare_fusion.47, pred[512,2048]{0,1:T(8,128)(4,1)S(1)} %get-tuple-element.1805, ...), kind=kOutput, calls=%fused_computation.139.clone.1 | convolution fusion | flops 468713472 | bytes 22003716 | tf_op jit(solution)/shard_map/while/body/eval_jaxpr/hqd,khd->hqk/dot_general | solution.py:233
  384.8 6.7 fusion.218
  411.0 110.1 %reduce-scatter.8.cloned.1.call-done = f32[512,384]{1,0:T(8,128)} async-done(((f32[4096,384]{1,0:T(8,128)}), f32[512,384]{1,0:T(8,128)}) %reduce-scatter.8.cloned.1.call-update) | async-done | bytes 786448 | tf_op jit(solution)/shard_map/reduce_scatter | solution.py:282
  536.3 9.7 %reduce-scatter.6.cloned.1.call-done = bf16[512,192]{0,1:T(8,128)(2,1)} async-done(((bf16[512,768]{0,1:T(8,128)(2,1)}), bf16[512,192]{0,1:T(8,128)(2,1)}) %reduce-scatter.6.cloned.1.call-update) | async-done | bytes 196624 | tf_op jit(solution)/shard_map/reduce_scatter | solution.py:176
  548.6 27.6 %all-gather.9.cloned.1.call-done = bf16[2048,768]{1,0:T(8,128)(2,1)} async-done(((bf16[512,768]{1,0:T(8,128)(2,1)}), bf16[2048,768]{1,0:T(8,128)(2,1)}) %all-gather.9.cloned.1.call-update) | async-done | bytes 3145744 | tf_op jit(solution)/shard_map/all_gather | solution.py:15
  584.6 40.6 %all-reduce = (f32[768]{0:T(1024)}, f32[768]{0:T(1024)}, f32[192]{0:T(256)}, f32[192]{0:T(256)}, f32[192]{0:T(256)}, /*index=5*/f32[192]{0:T(256)}, f32[768]{0:T...) all-reduce(f32[768]{0:T(1024)} %get-tuple-element.1285, ...), channel_id=1, replica_groups=mesh['seq'=8,'head'=4] {'seq'}, use_global_device_ids=true, to_apply=%region_36.37 | all-reduce | flops 6144 | bytes 49152 | tf_op jit(solution)/shard_map/psum | solution.py:302
  628.5 192.4 %all-reduce.9.cloned.1.call-done = (f32[768,192]{0,1:T(8,128)}, f32[768,192]{0,1:T(8,128)}, f32[768,192]{0,1:T(8,128)}, f32[192,768]{1,0:T(8,128)}, f32[768,768]{1,0:T(8,128)}, /*index=5*/f32[768,768]{1,0:T(8,128)}) async-done(((f32[768,192]{0,1:T(8,128)}, f32[768,192]{0,1:T(8,128)}, f32[768,192]{0,1:T(8,128)}, f32[192,768]{1,0:T(8,128)}, f32[768,768]{1,0:T(8,128)}, /*index=5*/f32[768,768]{1,0:T(8,128)}), ...) | async-done | bytes 7077904 | tf_op jit(solution)/shard_map/psum | solution.py:302
  (475 shorter events, 171.8 us)
Async XLA Ops:
  7.2 229.8 %copy-start = (bf16[768,768]{1,0:T(8,128)(2,1)S(1)}, bf16[768,768]{1,0:T(8,128)(2,1)}, u32[]{:S(2)}) copy-start(bf16[768,768]{1,0:T(8,128)(2,1)} %param.40) | copy-start | bytes 3538948
  7.2 59.4 %all-gather.5.cloned.1.call-start = ((), (), s32[]{:S(2)}) async-start(), calls=%async_computation.3 | async-start | bytes 1769472 | tf_op jit(solution)/shard_map/all_gather | solution.py:142
  20.3 92.5 %all-gather.7.cloned.1.call-start = ((), (), s32[]{:S(2)}) async-start(), calls=%async_computation.4 | async-start | bytes 1769472 | tf_op jit(solution)/shard_map/all_gather | solution.py:143
  21.4 204.1 %reduce-scatter.4.cloned.1.call-start = ((), (), s32[]{:S(2)}) async-start(), calls=%async_computation.5 | async-start | bytes 983040 | tf_op jit(solution)/shard_map/reduce_scatter | solution.py:162
  137.4 16.8 %copy-start.5 = (bf16[2,2048,3,64]{1,3,2,0:T(8,128)(2,1)S(1)}, bf16[2,2048,3,64]{1,3,2,0:T(8,128)(2,1)}, u32[]{:S(2)}) copy-start(bf16[2,2048,3,64]{1,3,2,0:T(8,128)(2,1)} %get-tuple-element.1868) | copy-start | bytes 4718596 | tf_op jit(solution)/shard_map/while
  176.3 16.8 %copy-start.5 = (bf16[2,2048,3,64]{1,3,2,0:T(8,128)(2,1)S(1)}, bf16[2,2048,3,64]{1,3,2,0:T(8,128)(2,1)}, u32[]{:S(2)}) copy-start(bf16[2,2048,3,64]{1,3,2,0:T(8,128)(2,1)} %get-tuple-element.1868) | copy-start | bytes 4718596 | tf_op jit(solution)/shard_map/while
  202.6 22.9 %copy-start.34 = (bf16[512,192]{0,1:T(8,128)(2,1)S(1)}, bf16[512,192]{0,1:T(8,128)(2,1)}, u32[]{:S(2)}) copy-start(bf16[512,192]{0,1:T(8,128)(2,1)} %param.24) | copy-start | bytes 589828
  204.1 76.6 %all-reduce.7.cloned.1.call-start = ((), (), s32[]{:S(2)}) async-start(), calls=%async_computation.7 | async-start | bytes 1572864 | tf_op jit(solution)/shard_map/psum | solution.py:193
  204.9 30.6 %copy-start.94 = (f32[192]{0:T(256)}, f32[192]{0:T(256)S(1)}, u32[]{:S(2)}) copy-start(f32[192]{0:T(256)S(1)} %dynamic_slice.65) | copy-start | bytes 2308
  213.5 23.4 %copy-start.23 = (bf16[512,768]{0,1:T(8,128)(2,1)}, bf16[512,768]{0,1:T(8,128)(2,1)S(1)}, u32[]{:S(2)}) copy-start(bf16[512,768]{0,1:T(8,128)(2,1)S(1)} %all_gather.27) | copy-start | bytes 2359300
  213.5 22.2 %copy-start.76 = (f32[768]{0:T(1024)S(1)}, f32[768]{0:T(1024)}, u32[]{:S(2)}) copy-start(f32[768]{0:T(1024)} %param.36) | copy-start | bytes 9220
  213.6 22.2 %copy-start.103 = (f32[768]{0:T(1024)S(1)}, f32[768]{0:T(1024)}, u32[]{:S(2)}) copy-start(f32[768]{0:T(1024)} %param.39) | copy-start | bytes 9220
  213.6 22.2 %copy-start.104 = (f32[768]{0:T(1024)S(1)}, f32[768]{0:T(1024)}, u32[]{:S(2)}) copy-start(f32[768]{0:T(1024)} %param.37) | copy-start | bytes 9220
  235.3 49.2 %copy-start.9 = (bf16[512,768]{0,1:T(8,128)(2,1)}, bf16[512,768]{0,1:T(8,128)(2,1)S(1)}, u32[]{:S(2)}) copy-start(bf16[512,768]{0,1:T(8,128)(2,1)S(1)} %all_gather.26) | copy-start | bytes 2359300
  235.5 49.1 %copy-start.74 = (f32[512]{0:T(512)}, f32[512]{0:T(512)S(1)}, u32[]{:S(2)}) copy-start(f32[512]{0:T(512)S(1)} %broadcast_multiply_fusion.1) | copy-start | bytes 6148
  235.8 48.8 %copy-start.83 = (f32[512]{0:T(512)}, f32[512]{0:T(512)S(1)}, u32[]{:S(2)}) copy-start(f32[512]{0:T(512)S(1)} %fusion.123) | copy-start | bytes 6148
  243.7 36.9 %copy-start.77 = (f32[768]{0:T(1024)S(1)}, f32[768]{0:T(1024)}, u32[]{:S(2)}) copy-start(f32[768]{0:T(1024)} %param.36) | copy-start | bytes 9220
  245.4 275.6 %reduce-scatter.8.cloned.1.call-start = ((), (), s32[]{:S(2)}) async-start(), calls=%async_computation.8 | async-start | bytes 7077888 | tf_op jit(solution)/shard_map/reduce_scatter | solution.py:282
  402.8 143.3 %reduce-scatter.6.cloned.1.call-start = ((), (), s32[]{:S(2)}) async-start(), calls=%async_computation.6 | async-start | bytes 983040 | tf_op jit(solution)/shard_map/reduce_scatter | solution.py:176
  408.4 167.8 %all-gather.9.cloned.1.call-start = ((), (), s32[]{:S(2)}) async-start(), calls=%async_computation.9 | async-start | bytes 3932160 | tf_op jit(solution)/shard_map/all_gather | solution.py:15
  409.4 112.9 %copy-start.43 = (bf16[768,192]{0,1:T(8,128)(2,1)S(1)}, bf16[768,192]{0,1:T(8,128)(2,1)}, u32[]{:S(2)}) copy-start(bf16[768,192]{0,1:T(8,128)(2,1)} %param.29) | copy-start | bytes 884740
  411.0 112.1 %copy-start.41 = (bf16[768,192]{0,1:T(8,128)(2,1)S(1)}, bf16[768,192]{0,1:T(8,128)(2,1)}, u32[]{:S(2)}) copy-start(bf16[768,192]{0,1:T(8,128)(2,1)} %param.30) | copy-start | bytes 884740
  524.5 296.4 %all-reduce.9.cloned.1.call-start = ((), (), s32[]{:S(2)}) async-start(), calls=%async_computation.10 | async-start | bytes 14155776 | tf_op jit(solution)/shard_map/psum | solution.py:302
  579.7 45.6 %copy-start.90 = (f32[512]{0:T(512)S(1)}, f32[512]{0:T(512)}, u32[]{:S(2)}) copy-start(f32[512]{0:T(512)} %copy-done.89) | copy-start | bytes 6148
  (121 other events, 632.8 us)
Sparse Core Ops, SparseCore 0:
  20.4 46.1 all-gather.4
  69.3 43.4 all-gather.6
  204.2 21.3 reduce-scatter.3
  245.6 35.0 all-reduce.6
  402.9 118.1 reduce-scatter.7
  523.6 22.4 reduce-scatter.5
  547.6 28.5 all-gather.8
  583.0 237.8 all-reduce.8
